TPU v7x, 256 devices: a whole 4x4x8 slice. The times are simulated.
256 devices in a mesh: seq: 8 (over x, core), exp: 32 (over y, z).
Axes of the slice: x: 4, y: 4, z: 8, core: 2. Of those that a mesh axis runs over, the one named last changes fastest.
Arguments:
- tokens: bfloat16 [4096, 7168], P('exp', 'seq'), may hold values from -6 to 6
- out_grad: bfloat16 [4096, 7168], P('exp', 'seq'), may hold values from -6 to 6
- expert_ids: int32 [4096, 8], P('exp'), may hold values from 0 to 255, as said below
- route_weights: float32 [4096, 8], P('exp'), may hold values from 0.2 to 2.5
- gate_proj: bfloat16 [32, 7168, 2048], P('exp', None, 'seq'), may hold values from -0.0625 to 0.0625
- up_proj: bfloat16 [32, 7168, 2048], P('exp', None, 'seq'), may hold values from -0.0625 to 0.0625
- down_proj: bfloat16 [32, 2048, 7168], P('exp', 'seq'), may hold values from -0.125 to 0.125
Outputs:
- token_grad: bfloat16 [4096, 7168], P('exp', 'seq')
- route_grad: float32 [4096, 8], P('exp', 'seq')
Inputs may be any that keep to these rules, and one draw needn't show every extreme that they name: `expert_ids`: each row names 8 different experts, at most one of them below 32; between 96 and all of the 128 rows of one index of exp name one below 32; those rows name any one expert below 32 at most 8 times, and in every draw one such expert exactly 8 times on every index of exp.
All inputs are finite; a program needn't handle non-finite values.
Results may differ from a plain program's by a relative error of at most 0.0049.
Values may be sent and summed in bfloat16 or wider, within the bound.
A program may use at most 128 MiB of HBM per device.

v0:
```python
import jax
import jax.numpy as jnp
from jax import lax
from jax.sharding import PartitionSpec as P

PRECISE = lax.Precision.HIGHEST
CONTRACT = (((1,), (1,)), ((), ()))


def expert_front(row_inputs, row_grads, w_gate, w_up, w_down):
    pre_gate = jnp.dot(row_inputs, w_gate, preferred_element_type=jnp.float32)
    pre_up = jnp.dot(row_inputs, w_up, preferred_element_type=jnp.float32)
    back_grad = lax.dot_general(row_grads, w_down, CONTRACT, preferred_element_type=jnp.float32)
    gate_sig = jax.nn.sigmoid(pre_gate)
    active = pre_gate * gate_sig
    route_part = jnp.sum(active * pre_up * back_grad, axis=-1)
    grad_gate = (back_grad * pre_up * gate_sig * (1.0 + pre_gate * (1.0 - gate_sig))).astype(
        jnp.bfloat16
    )
    grad_up = (back_grad * active).astype(jnp.bfloat16)
    return (grad_gate, grad_up, route_part)


def expert_back(grad_gate, grad_up, w_gate, w_up):
    return lax.dot_general(
        grad_gate, w_gate, CONTRACT, preferred_element_type=jnp.float32
    ) + lax.dot_general(grad_up, w_up, CONTRACT, preferred_element_type=jnp.float32)


def slot_match(route_ids, most_rows, slot_count):
    expert_total = slot_count // most_rows
    named_hot = (route_ids[..., None] == jnp.arange(expert_total, dtype=jnp.int32)).astype(
        jnp.int32
    )
    per_token = jnp.sum(named_hot, axis=1)
    earlier = jnp.cumsum(per_token, axis=0) - per_token
    slot_rank = jnp.sum(named_hot * earlier[:, None, :], axis=-1)
    target = route_ids * most_rows + slot_rank
    return target[..., None] == jnp.arange(slot_count, dtype=jnp.int32)


def local(tokens, out_grad, expert_ids, route_weights, gate_proj, up_proj, down_proj):
    exp_count = lax.axis_size("exp")
    tok_dev = tokens.shape[0]
    expert_count = exp_count * gate_proj.shape[0]
    most_rows = max(2, 2 * ((tok_dev + expert_count - 1) // expert_count))
    slot_count = expert_count * most_rows
    w_gate = gate_proj[0]
    w_up = up_proj[0]
    w_down = down_proj[0]
    full_x, full_dy = (
        lax.all_gather(tokens, "seq", axis=1, tiled=True),
        lax.all_gather(out_grad, "seq", axis=1, tiled=True),
    )
    model_width = full_x.shape[1]
    matched = slot_match(expert_ids, most_rows, slot_count)
    selector = jnp.sum(matched, axis=1).astype(jnp.bfloat16)
    both_rows = jnp.concatenate([full_x, full_dy], axis=1)
    packed = jnp.einsum(
        "ts,td->sd", selector, both_rows, preferred_element_type=jnp.float32
    ).astype(jnp.bfloat16)
    packed = packed.reshape(expert_count, most_rows, 2 * model_width)
    weighted = jnp.sum(jnp.where(matched, route_weights[..., None], 0.0), axis=1)
    matched_float = matched.astype(jnp.float32)
    arrived = lax.all_to_all(packed, "exp", split_axis=0, concat_axis=0, tiled=True)
    layout = arrived.shape
    flat_rows = arrived.reshape(-1, layout[2])
    grad_gate, grad_up, route_part = expert_front(
        flat_rows[:, :model_width], flat_rows[:, model_width:], w_gate, w_up, w_down
    )
    slot_grad = expert_back(grad_gate, grad_up, w_gate, w_up).reshape(
        layout[0], layout[1], model_width
    )
    back_grad = lax.all_to_all(slot_grad, "exp", split_axis=0, concat_axis=0, tiled=True)
    back_route = lax.all_to_all(
        route_part.reshape(layout[0], layout[1]), "exp", split_axis=0, concat_axis=0, tiled=True
    )
    token_part = jnp.dot(weighted, back_grad.reshape(slot_count, model_width), precision=PRECISE)
    route_part = jnp.einsum(
        "tks,s->tk", matched_float, back_route.reshape(slot_count), precision=PRECISE
    )
    own_grad, own_route = (
        lax.psum_scatter(token_part, "seq", scatter_dimension=1, tiled=True),
        lax.psum_scatter(route_part, "seq", scatter_dimension=1, tiled=True),
    )
    return (own_grad.astype(jnp.bfloat16), own_route)


def solution(mesh):
    in_specs = (
        P("exp", "seq"),
        P("exp", "seq"),
        P("exp", None),
        P("exp", None),
        P("exp", None, "seq"),
        P("exp", None, "seq"),
        P("exp", "seq", None),
    )
    out_specs = (P("exp", "seq"), P("exp", "seq"))
    return jax.shard_map(local, mesh=mesh, in_specs=in_specs, out_specs=out_specs, check_vma=False)
```

profile of v0, /device:TPU:8, one launch (start us, length us, event | category | flops | bytes accessed | tf_op | source)
XLA Modules:
  0.0 482.7 jit_solution(10725312584192944092)
XLA Ops:
  7.2 0.0 all-gather.3.cloned.1.call-start
  7.2 0.7 all-gather.3.cloned.1.call-update
  7.9 0.0 all-gather.5.cloned.1.call-start
  7.9 0.7 all-gather.5.cloned.1.call-update
  8.6 0.7 convert_reduce_fusion.1
  9.4 0.1 copy.19
  9.5 0.2 reduce_window_sum.11
  9.6 0.1 copy.21
  9.7 0.7 select_reduce_fusion.1
  10.4 0.7 multiply_add_fusion
  11.1 0.1 copy.22
  11.2 0.4 convert_reduce_fusion
  11.6 28.5 %all-gather.3.cloned.1.call-done = bf16[128,7168]{1,0:T(8,128)(2,1)} async-done(((bf16[128,896]{1,0:T(8,128)(2,1)}), bf16[128,7168]{1,0:T(8,128)(2,1)}) %all-gather.3.cloned.1.call-update) | async-done | bytes 1835024 | tf_op jit(solution)/shard_map/all_gather | solution.py:52
  40.2 29.5 %all-gather.5.cloned.1.call-done = bf16[128,7168]{1,0:T(8,128)(2,1)} async-done(((bf16[128,896]{1,0:T(8,128)(2,1)}), bf16[128,7168]{1,0:T(8,128)(2,1)}) %all-gather.5.cloned.1.call-update) | async-done | bytes 1835024 | tf_op jit(solution)/shard_map/all_gather | solution.py:53
  69.7 4.1 fusion
  73.8 0.0 copy-start.1
  73.8 171.5 %all_to_all.19 = bf16[32,8,14336]{2,1,0:T(8,128)(2,1)S(1)} all-to-all(bf16[32,8,14336]{2,1,0:T(8,128)(2,1)S(1)} %fusion), channel_id=1, replica_groups=mesh['seq'=8,'exp'=32] {'exp'}, dimensions={0} | all-to-all | bytes 14680064 | tf_op jit(solution)/shard_map/all_to_all | solution.py:65
  245.4 0.0 copy-done.1
  245.4 0.0 copy-start
  245.4 1.6 fusion.11
  247.0 0.4 copy-done
  247.4 0.0 copy-start.3
  247.4 1.6 fusion.14
  249.0 0.4 copy-done.3
  249.5 1.2 multiply_reduce_fusion
  250.6 1.2 fusion.9
  251.9 4.2 fusion.1
  256.1 0.0 copy-start.2
  256.1 7.8 %all-to-all-start.1 = ((f32[32,8,7168]{2,1,0:T(8,128)}), f32[32,8,7168]{2,1,0:T(8,128)}, u32[]{:S(2)}, u32[]{:S(2)}) async-start(f32[32,8,7168]{2,1,0:T(8,128)} %fusion.1), calls=%async_computation.1 | async-start | bytes 14680064 | tf_op jit(solution)/shard_map/all_to_all | solution.py:74
  263.9 0.2 reduce-scatter.2.cloned.1.call-start
  264.1 0.0 copy-done.2
  264.2 0.1 copy.23
  264.3 0.4 select_reduce_fusion
  264.6 160.9 %all-to-all-done.1 = f32[32,8,7168]{2,1,0:T(8,128)} async-done(((f32[32,8,7168]{2,1,0:T(8,128)}), f32[32,8,7168]{2,1,0:T(8,128)}, u32[]{:S(2)}, u32[]{:S(2)}) %all-to-all-start.1) | async-done | bytes 7340064 | tf_op jit(solution)/shard_map/all_to_all | solution.py:74
  425.5 9.1 %fusion.2 = f32[128,7168]{1,0:T(8,128)} fusion(f32[128,256]{1,0:T(8,128)S(1)} %select_reduce_fusion, f32[32,8,7168]{2,1,0:T(8,128)} %all-to-all-done.1), kind=kOutput, calls=%fused_computation.4 | convolution fusion | flops 2818572288 | bytes 11141120 | tf_op jit(solution)/shard_map/dot_general | solution.py:78
  434.6 0.0 copy-start.4
  434.6 0.0 reduce-scatter.2.cloned.1.call-update
  434.7 0.7 all_to_all.14
  435.4 9.9 %all-to-all-start.2 = ((f32[32,1,8]{2,1,0:T(1,128)}), f32[32,1,8]{2,1,0:T(1,128)S(1)}, u32[]{:S(2)}, u32[]{:S(2)}) async-start(f32[32,1,8]{2,1,0:T(1,128)} %bitcast.7), calls=%async_computation.3 | async-start | bytes 32768 | tf_op jit(solution)/shard_map/all_to_all | solution.py:75
  445.3 0.0 copy-done.4
  445.3 0.6 dynamic-slice
  445.9 7.9 %all-to-all-done.2 = f32[32,1,8]{2,1,0:T(1,128)S(1)} async-done(((f32[32,1,8]{2,1,0:T(1,128)}), f32[32,1,8]{2,1,0:T(1,128)S(1)}, u32[]{:S(2)}, u32[]{:S(2)}) %all-to-all-start.2) | async-done | bytes 1056 | tf_op jit(solution)/shard_map/all_to_all | solution.py:75
  453.8 0.5 broadcast.25
  454.3 0.7 reduce.3
  455.0 0.1 reshape.41
  455.1 3.6 fusion.19
  458.8 0.1 copy.25
  458.8 12.5 %all-reduce = f32[128,8]{0,1:T(8,128)S(1)} all-reduce(f32[128,8]{0,1:T(8,128)S(1)} %bitcast.31), channel_id=3, replica_groups=mesh['seq'=8,'exp'=32] {'seq'}, use_global_device_ids=true, to_apply=%region_7.8.clone | all-reduce | flops 1024 | bytes 8192
  471.4 1.2 constant_dynamic-slice_fusion
  472.5 1.9 reduce-scatter.2.cloned.1.call-done
  474.4 1.7 convert_element_type.28
  (1 shorter events, 0.0 us)
Async XLA Ops:
  7.2 33.0 %all-gather.3.cloned.1.call-start = ((), (), s32[]{:S(2)}) async-start(), calls=%async_computation.4 | async-start | bytes 2064384 | tf_op jit(solution)/shard_map/all_gather | solution.py:52
  7.9 61.8 %all-gather.5.cloned.1.call-start = ((), (), s32[]{:S(2)}) async-start(), calls=%async_computation.5 | async-start | bytes 2064384 | tf_op jit(solution)/shard_map/all_gather | solution.py:53
  73.8 171.5 %copy-start.1 = (bf16[1,7168,256]{2,1,0:T(8,128)(2,1)S(1)}, bf16[1,7168,256]{2,1,0:T(8,128)(2,1)}, u32[]{:S(2)}) copy-start(bf16[1,7168,256]{2,1,0:T(8,128)(2,1)} %param.11) | copy-start | bytes 11010052
  245.4 2.0 copy-start
  247.4 2.0 copy-start.3
  256.1 8.0 %copy-start.2 = (f32[128,8]{0,1:T(8,128)S(1)}, f32[128,8]{0,1:T(8,128)}, u32[]{:S(2)}) copy-start(f32[128,8]{0,1:T(8,128)} %param.10) | copy-start | bytes 12292
  256.1 169.4 %all-to-all-start.1 = ((f32[32,8,7168]{2,1,0:T(8,128)}), f32[32,8,7168]{2,1,0:T(8,128)}, u32[]{:S(2)}, u32[]{:S(2)}) async-start(f32[32,8,7168]{2,1,0:T(8,128)} %fusion.1), calls=%async_computation.1 | async-start | bytes 14680064 | tf_op jit(solution)/shard_map/all_to_all | solution.py:74
  263.9 210.5 %reduce-scatter.2.cloned.1.call-start = ((), (), s32[]{:S(2)}) async-start(), calls=%async_computation.6 | async-start | bytes 4128768 | tf_op jit(solution)/shard_map/reduce_scatter | solution.py:83
  434.6 10.6 %copy-start.4 = (u32[256]{0:T(256)S(1)}, u32[256]{0:T(256)}, u32[]{:S(2)}) copy-start(u32[256]{0:T(256)} %constant.17) | copy-start | bytes 3076
  435.4 18.5 %all-to-all-start.2 = ((f32[32,1,8]{2,1,0:T(1,128)}), f32[32,1,8]{2,1,0:T(1,128)S(1)}, u32[]{:S(2)}, u32[]{:S(2)}) async-start(f32[32,1,8]{2,1,0:T(1,128)} %bitcast.7), calls=%async_computation.3 | async-start | bytes 32768 | tf_op jit(solution)/shard_map/all_to_all | solution.py:75
Sparse Core Ops, SparseCore 0:
  9.8 30.2 all-gather.2
  42.0 27.6 all-gather.4
  434.8 39.5 reduce-scatter.1
where the time goes:
time: 483 us
  waiting for transfers between devices  230 us (48%)
  blocking collectives  184 us (38%)
  matrix products  26.7 us (6%)
  starting transfers between devices  18 us (4%)
  between operations  13.9 us (3%)
  other arithmetic  5.49 us (1%)
    all_to_all x1, blocking collectives, local(): lax.all_to_all(packed, 'exp', split_axis=0, concat_axis=0, tiled=True)  172 us
    all_to_all x1, waiting for transfers between devices, local(): lax.all_to_all(slot_grad, 'exp', split_axis=0, concat_axis=0, tiled=True)  161 us
    all_gather x1, waiting for transfers between devices, local(): lax.all_gather(out_grad, 'seq', axis=1, tiled=True)  29.5 us
    all_gather x1, waiting for transfers between devices, local(): lax.all_gather(tokens, 'seq', axis=1, tiled=True)  28.5 us
    unnamed x1, blocking collectives  12.5 us
    all_to_all x1, starting transfers between devices, local(): lax.all_to_all(route_part.reshape(layout[0], layout[1]), 'exp', split_axi...  9.9 us
  transfers between devices with their start and end apart: 5, of which 5 were waited for; matrix products, arithmetic and copies ran while one was open for 2% of the time, Pallas kernels for 0%

commit v1 on v0

--- a/solution.py
+++ b/solution.py
@@ -50,7 +50,9 @@
     w_down = down_proj[0]
     full_x, full_dy = (
         lax.all_gather(tokens, "seq", axis=1, tiled=True),
-        lax.all_gather(out_grad, "seq", axis=1, tiled=True),
+        jnp.concatenate(
+            lax.all_to_all(jnp.stack([out_grad] * lax.axis_size("seq")), "seq", 0, 0), axis=1
+        ),
     )
     model_width = full_x.shape[1]
     matched = slot_match(expert_ids, most_rows, slot_count)

time: 483 us -> 464 us (0.961)
  waiting for transfers between devices: 230 us -> 200 us
  local copies, waits for them, and re-layouts: 4.42 us -> 11 us
    all_to_all x0 -> x1, waiting for transfers between devices: none -> 30.8 us  [local(): lax.all_to_all(jnp.stack([out_grad] * lax.axis_size('seq')), 'seq', 0, 0)]
    all_gather x1 -> x0, waiting for transfers between devices: 29.5 us -> none  [local(): lax.all_gather(out_grad, 'seq', axis=1, tiled=True)]
    all_gather x1, waiting for transfers between devices: 28.5 us -> 0.01 us  [local(): lax.all_gather(tokens, 'seq', axis=1, tiled=True)]
  transfers between devices with their start and end apart: 5 -> 5, of which waited for: 5 -> 4; matrix products, arithmetic and copies ran while one was open for 2% -> 3% of each run, Pallas kernels for 0% -> 0%
where the time goes in v1:
time: 464 us; the launch traced here: 463 us
  waiting for transfers between devices  200 us (43%)
  blocking collectives  185 us (40%)
  matrix products  26.7 us (6%)
  starting transfers between devices  22.5 us (5%)
  between operations  14.2 us (3%)
  local copies, waits for them, and re-layouts  11 us (2%)
    all_to_all x1, blocking collectives, local(): lax.all_to_all(packed, 'exp', split_axis=0, concat_axis=0, tiled=True)  173 us
    all_to_all x1, waiting for transfers between devices, local(): lax.all_to_all(slot_grad, 'exp', split_axis=0, concat_axis=0, tiled=True)  160 us
    all_to_all x1, waiting for transfers between devices, local(): lax.all_to_all(jnp.stack([out_grad] * lax.axis_size('seq')), 'seq', 0, 0)  30.8 us
    unnamed x1, blocking collectives  12.7 us
    all_to_all x1, starting transfers between devices, local(): lax.all_to_all(route_part.reshape(layout[0], layout[1]), 'exp', split_axi...  10.4 us
  transfers between devices with their start and end apart: 5, of which 4 were waited for; matrix products, arithmetic and copies ran while one was open for 3% of the time, Pallas kernels for 0%

profile of v1, /device:TPU:8, one launch (start us, length us, event | category | flops | bytes accessed | tf_op | source)
XLA Modules:
  0.0 463.4 jit_solution(879313617349607932)
XLA Ops:
  7.2 0.0 copy-start.2
  7.2 0.0 all-gather.2.cloned.1.call-start
  7.2 1.8 copy.30
  9.0 0.0 all-gather.2.cloned.1.call-update
  9.0 2.4 stack.2
  11.4 4.3 all-to-all-start
  15.7 0.0 copy-done.2
  15.7 0.1 copy.25
  15.8 0.2 reduce_window_sum.11
  16.0 0.1 copy.27
  16.1 0.1 copy.28
  16.3 0.4 convert_reduce_fusion
  16.6 30.8 %all-to-all-done = bf16[8,128,896]{2,1,0:T(8,128)(2,1)S(1)} async-done(((bf16[8,128,896]{2,1,0:T(8,128)(2,1)}), bf16[8,128,896]{2,1,0:T(8,128)(2,1)S(1)}, u32[]{:S(2)}, u32[]{:S(2)}) %all-to-all-start) | async-done | bytes 1835040 | tf_op jit(solution)/shard_map/all_to_all | solution.py:54
  47.4 2.4 copy.31
  49.8 0.0 all-gather.2.cloned.1.call-done
  49.8 4.1 fusion
  54.0 0.0 copy-start.1
  54.0 172.7 %all_to_all.24 = bf16[32,8,14336]{2,1,0:T(8,128)(2,1)S(1)} all-to-all(bf16[32,8,14336]{2,1,0:T(8,128)(2,1)S(1)} %fusion), channel_id=1, replica_groups=mesh['seq'=8,'exp'=32] {'exp'}, dimensions={0} | all-to-all | bytes 14680064 | tf_op jit(solution)/shard_map/all_to_all | solution.py:67
  226.7 0.0 copy-done.1
  226.7 0.0 copy-start
  226.7 1.6 fusion.11
  228.3 0.4 copy-done
  228.7 0.0 copy-start.4
  228.8 1.6 fusion.14
  230.4 0.4 copy-done.4
  230.8 1.2 multiply_reduce_fusion
  232.0 1.2 fusion.9
  233.2 4.2 fusion.1
  237.4 0.0 copy-start.3
  237.4 7.5 %all-to-all-start.2 = ((f32[32,8,7168]{2,1,0:T(8,128)}), f32[32,8,7168]{2,1,0:T(8,128)}, u32[]{:S(2)}, u32[]{:S(2)}) async-start(f32[32,8,7168]{2,1,0:T(8,128)} %fusion.1), calls=%async_computation.2 | async-start | bytes 14680064 | tf_op jit(solution)/shard_map/all_to_all | solution.py:76
  244.9 0.2 reduce-scatter.2.cloned.1.call-start
  245.1 0.0 copy-done.3
  245.2 0.1 copy.29
  245.3 0.4 select_reduce_fusion
  245.6 160.4 %all-to-all-done.2 = f32[32,8,7168]{2,1,0:T(8,128)} async-done(((f32[32,8,7168]{2,1,0:T(8,128)}), f32[32,8,7168]{2,1,0:T(8,128)}, u32[]{:S(2)}, u32[]{:S(2)}) %all-to-all-start.2) | async-done | bytes 7340064 | tf_op jit(solution)/shard_map/all_to_all | solution.py:76
  406.0 9.1 %fusion.2 = f32[128,7168]{1,0:T(8,128)} fusion(f32[128,256]{1,0:T(8,128)S(1)} %select_reduce_fusion, f32[32,8,7168]{2,1,0:T(8,128)} %all-to-all-done.2), kind=kOutput, calls=%fused_computation.4 | convolution fusion | flops 2818572288 | bytes 11141120 | tf_op jit(solution)/shard_map/dot_general | solution.py:80
  415.2 0.0 copy-start.5
  415.2 0.0 reduce-scatter.2.cloned.1.call-update
  415.2 0.7 all_to_all.18
  415.9 10.4 %all-to-all-start.3 = ((f32[32,1,8]{2,1,0:T(1,128)}), f32[32,1,8]{2,1,0:T(1,128)S(1)}, u32[]{:S(2)}, u32[]{:S(2)}) async-start(f32[32,1,8]{2,1,0:T(1,128)} %bitcast.9), calls=%async_computation.4 | async-start | bytes 32768 | tf_op jit(solution)/shard_map/all_to_all | solution.py:77
  426.3 0.0 copy-done.5
  426.3 0.6 dynamic-slice
  427.0 7.9 %all-to-all-done.3 = f32[32,1,8]{2,1,0:T(1,128)S(1)} async-done(((f32[32,1,8]{2,1,0:T(1,128)}), f32[32,1,8]{2,1,0:T(1,128)S(1)}, u32[]{:S(2)}, u32[]{:S(2)}) %all-to-all-start.3) | async-done | bytes 1056 | tf_op jit(solution)/shard_map/all_to_all | solution.py:77
  434.9 0.5 broadcast.27
  435.4 0.7 reduce.3
  436.1 0.1 reshape.51
  436.2 3.6 fusion.19
  439.8 0.1 copy.33
  439.9 12.7 %all-reduce = f32[128,8]{0,1:T(8,128)S(1)} all-reduce(f32[128,8]{0,1:T(8,128)S(1)} %bitcast.35), channel_id=3, replica_groups=mesh['seq'=8,'exp'=32] {'seq'}, use_global_device_ids=true, to_apply=%region_7.8.clone | all-reduce | flops 1024 | bytes 8192
  452.5 1.2 constant_dynamic-slice_fusion
  453.7 1.2 reduce-scatter.2.cloned.1.call-done
  454.9 1.7 convert_element_type.28
  (4 shorter events, 0.1 us)
Async XLA Ops:
  7.2 8.6 %copy-start.2 = (s32[128,8]{0,1:T(8,128)S(1)}, s32[128,8]{0,1:T(8,128)}, u32[]{:S(2)}) copy-start(s32[128,8]{0,1:T(8,128)} %param.9) | copy-start | bytes 12292
  7.2 42.7 %all-gather.2.cloned.1.call-start = ((), (), s32[]{:S(2)}) async-start(), calls=%async_computation.5 | async-start | bytes 2064384 | tf_op jit(solution)/shard_map/all_gather | solution.py:52
  11.4 36.0 %all-to-all-start = ((bf16[8,128,896]{2,1,0:T(8,128)(2,1)}), bf16[8,128,896]{2,1,0:T(8,128)(2,1)S(1)}, u32[]{:S(2)}, u32[]{:S(2)}) async-start(bf16[8,128,896]{2,1,0:T(8,128)(2,1)} %stack.2), calls=%async_computation | async-start | bytes 3670016 | tf_op jit(solution)/shard_map/all_to_all | solution.py:54
  54.0 172.7 %copy-start.1 = (bf16[1,7168,256]{2,1,0:T(8,128)(2,1)S(1)}, bf16[1,7168,256]{2,1,0:T(8,128)(2,1)}, u32[]{:S(2)}) copy-start(bf16[1,7168,256]{2,1,0:T(8,128)(2,1)} %param.11) | copy-start | bytes 11010052
  226.7 2.0 copy-start
  228.7 2.0 copy-start.4
  237.4 7.7 %copy-start.3 = (f32[128,8]{0,1:T(8,128)S(1)}, f32[128,8]{0,1:T(8,128)}, u32[]{:S(2)}) copy-start(f32[128,8]{0,1:T(8,128)} %param.10) | copy-start | bytes 12292
  237.4 168.6 %all-to-all-start.2 = ((f32[32,8,7168]{2,1,0:T(8,128)}), f32[32,8,7168]{2,1,0:T(8,128)}, u32[]{:S(2)}, u32[]{:S(2)}) async-start(f32[32,8,7168]{2,1,0:T(8,128)} %fusion.1), calls=%async_computation.2 | async-start | bytes 14680064 | tf_op jit(solution)/shard_map/all_to_all | solution.py:76
  244.9 210.0 %reduce-scatter.2.cloned.1.call-start = ((), (), s32[]{:S(2)}) async-start(), calls=%async_computation.6 | async-start | bytes 4128768 | tf_op jit(solution)/shard_map/reduce_scatter | solution.py:85
  415.2 11.2 %copy-start.5 = (u32[256]{0:T(256)S(1)}, u32[256]{0:T(256)}, u32[]{:S(2)}) copy-start(u32[256]{0:T(256)} %constant.17) | copy-start | bytes 3076
  415.9 19.0 %all-to-all-start.3 = ((f32[32,1,8]{2,1,0:T(1,128)}), f32[32,1,8]{2,1,0:T(1,128)S(1)}, u32[]{:S(2)}, u32[]{:S(2)}) async-start(f32[32,1,8]{2,1,0:T(1,128)} %bitcast.9), calls=%async_computation.4 | async-start | bytes 32768 | tf_op jit(solution)/shard_map/all_to_all | solution.py:77
Sparse Core Ops, SparseCore 0:
  10.4 34.8 all-gather.1
  415.3 39.5 reduce-scatter.1
